TPU v7x, 256 devices: a whole 4x4x8 slice. The times are simulated.
256 devices in a mesh: gx: 8 (over z), gy: 32 (over y, x, core).
Axes of the slice: x: 4, y: 4, z: 8, core: 2. Of those that a mesh axis runs over, the one named last changes fastest.
Arguments:
- coupling: bfloat16 [8, 256, 1024, 512], P('gx', 'gy'), may hold values from -0.44921875 to 0.44921875
- local_block: bfloat16 [8, 256, 512, 512], P('gx', 'gy'), as said below
- counts: int32 [8, 256], P('gx', 'gy'), may hold values from 1 to 4, as said below
- primal: int32 [8, 256, 512], P('gx', 'gy'), may hold values from 0 to 511
- partner: int32 [3, 8], replicated, may hold values from 0 to 7, as said below
Outputs:
- coarse: float32 [8, 512, 512], P('gx')
Inputs may be any that keep to these rules, and one draw needn't show every extreme that they name: Each row of partner is a perfect matching of the 8 columns: partner[r, partner[r, c]] == c and partner[r, c] != c. `counts`: in each subdomain column at least one subdomain has all 4 blocks live. `primal`: any constraint may hold any number of rows. `local_block`: diagonal entries are positive.
All inputs are finite; a program needn't handle non-finite values. Where the computation divides by a largest or mean magnitude, that divisor is 1e-20 or more.
Results may differ from a plain program's by a relative error of at most 0.00078.
Values sent between devices are 32-bit elements; how exact they have to be, the bound alone decides.
A program may use at most 192 MiB of HBM per device.

v0:
```python
import jax
import jax.numpy as jnp
from jax import lax
from jax.sharding import PartitionSpec as P

BLK = 128
NC = 512
ROUNDS = 3
R = 512


def per_device(coupling, local_block, counts, primal, partner):
    column = lax.axis_index("gx")
    stiff = jnp.diagonal(local_block[0], axis1=1, axis2=2).astype(jnp.float32)
    total = stiff
    for r in range(ROUNDS):
        mate = partner[r, column]
        piece = jax.tree.map(
            lambda part: lax.all_gather(part, "gx", axis=0, tiled=True), stiff[None]
        )
        index = jnp.arange(piece.shape[0], dtype=jnp.int32)
        hit = (index == mate)[:, None, None]
        total = total + (
            jnp.zeros_like(stiff)
            + jnp.sum(jnp.where(hit, piece, jnp.zeros((), jnp.float32)), axis=0)
        )
    weight = stiff / total
    rows = jnp.arange(R, dtype=jnp.int32)
    live = (rows[None, :] < counts[0][:, None] * BLK).astype(jnp.float32)
    gram = jnp.einsum("snr,snq->srq", coupling[0], coupling[0], preferred_element_type=jnp.float32)
    schur = (
        (local_block[0].astype(jnp.float32) - gram) * live[:, :, None] * live[:, None, :]
    ).astype(jnp.bfloat16)
    onehot = primal[0][:, :, None] == jnp.arange(NC, dtype=jnp.int32)[None, None, :]
    basis = jnp.where(onehot, weight[:, :, None], jnp.zeros((), jnp.float32)).astype(jnp.bfloat16)
    image = jnp.einsum("srq,sqk->srk", schur, basis, preferred_element_type=jnp.float32).astype(
        jnp.bfloat16
    )
    tile = jnp.einsum("srk,srl->kl", basis, image, preferred_element_type=jnp.float32)
    summed = lax.psum(tile, "gy")
    scale = 1.0 / jnp.sqrt(jnp.mean(jnp.abs(summed), axis=1) + 1e-06)
    result = summed * scale[:, None] * scale[None, :]
    return result[None]


def solution(mesh):
    placed = (
        P("gx", "gy", None, None),
        P("gx", "gy", None, None),
        P("gx", "gy"),
        P("gx", "gy", None),
        P(),
    )
    return jax.shard_map(
        per_device, mesh=mesh, in_specs=placed, out_specs=P("gx", None, None), check_vma=False
    )
```

profile of v0, /device:TPU:1, one launch (start us, length us, event | category | flops | bytes accessed | tf_op | source)
XLA Modules:
  0.0 238.6 jit_solution(16034111459191862440)
XLA Ops:
  6.5 0.0 all-reduce.2.cloned.1.call-start
  6.5 1.5 constant_dynamic-slice_fusion
  8.0 0.7 iota_compare_fusion.4
  8.7 44.1 %copy.19 = bf16[8,512,512]{0,2,1:T(8,128)(2,1)} copy(bf16[8,512,512]{2,1,0:T(8,128)(2,1)} %bitcast.35) | data formatting | bytes 8388608 | tf_op jit(solution)/shard_map/squeeze | solution.py:14
  52.8 6.5 %gather_fusion = bf16[512,8]{1,0:T(8,128)(2,1)S(1)} fusion(bf16[8,512,512]{0,2,1:T(8,128)(2,1)} %copy.19, s32[512]{0:T(512)S(1)} %bitcast.34), kind=kCustom, calls=%fused_computation | custom fusion | bytes 20480 | tf_op jit(solution)/shard_map/jit(diagonal)/gather | solution.py:14
  59.3 0.1 copy.20
  59.3 23.0 %all-gather = f32[64,512]{1,0:T(8,128)S(1)} all-gather(f32[8,512]{1,0:T(8,128)S(1)} %convert_bitcast_fusion), channel_id=2, replica_groups=mesh['gx'=8,'gy'=32] {'gx'}, dimensions={0}, use_global_device_ids=true | all-gather | bytes 147456 | tf_op jit(solution)/shard_map/all_gather | solution.py:19
  82.4 0.0 copy-start.1
  82.4 0.0 copy-start
  82.4 13.6 %fusion = f32[8,512,512]{2,1,0:T(8,128)} fusion(bf16[1,8,1024,512]{3,2,1,0:T(8,128)(2,1)} %param.5), kind=kOutput, calls=%fused_computation.1 | convolution fusion | flops 4294967296 | bytes 16777216 | tf_op jit(solution)/shard_map/snr,snq->srq/dot_general | solution.py:30
  95.9 0.0 copy-done.1
  95.9 0.1 fusion.21
  96.0 1.2 iota_compare_fusion.2
  97.2 0.1 fusion.18
  97.4 0.0 copy-done
  97.4 10.2 %fusion.15 = f32[512,512]{1,0:T(8,128)} fusion(f32[8,512,512]{2,1,0:T(8,128)} %fusion, f32[8,512]{1,0:T(8,128)S(1)} %fusion.21, bf16[8,512]{1,0:T(8,128)(2,1)S(1)} %add_divide_fusion, s32[8,512]{1,0:T(8,128)S(1)} %bitcast.36, bf16[1,8,512,512]{3,2,1,0:T(8,128)(2,1)} %param.6), kind=kOutput, calls=%fused_computation.14 | convolution fusion | flops 4315938816 | bytes 13672448 | tf_op jit(solution)/shard_map/srk,srl->kl/dot_general | solution.py:39
  107.6 0.0 all-reduce.2.cloned.1.call-update
  107.6 120.4 %all-reduce.2.cloned.1.call-done = f32[512,512]{1,0:T(8,128)} async-done(((f32[512,512]{1,0:T(8,128)}), f32[512,512]{1,0:T(8,128)}) %all-reduce.2.cloned.1.call-update) | async-done | bytes 1048592 | tf_op jit(solution)/shard_map/psum | solution.py:40
  228.0 1.4 abs_reduce_fusion
  229.4 2.4 multiply_bitcast_fusion
  (5 shorter events, 0.0 us)
Async XLA Ops:
  6.5 221.5 %all-reduce.2.cloned.1.call-start = ((), (), s32[]{:S(2)}) async-start(), calls=%async_computation | async-start | bytes 2097152 | tf_op jit(solution)/shard_map/psum | solution.py:40
  82.4 13.6 %copy-start.1 = (s32[1,8]{1,0:T(1,128)S(1)}, s32[1,8]{1,0:T(1,128)}, u32[]{:S(2)}) copy-start(s32[1,8]{1,0:T(1,128)} %param.7) | copy-start | bytes 100
  82.4 15.0 %copy-start = (s32[1,8,512]{2,1,0:T(8,128)S(1)}, s32[1,8,512]{2,1,0:T(8,128)}, u32[]{:S(2)}) copy-start(s32[1,8,512]{2,1,0:T(8,128)} %param.8) | copy-start | bytes 49156
Sparse Core Ops, SparseCore 0:
  107.7 120.2 all-reduce.1
where the time goes:
time: 241 us; the launch traced here: 239 us
  waiting for transfers between devices  120 us (50%)
  local copies, waits for them, and re-layouts  52.1 us (22%)
  matrix products  23.7 us (10%)
  blocking collectives  23 us (10%)
  between operations  13.4 us (6%)
  other arithmetic  5.85 us (2%)
    psum x1, waiting for transfers between devices, per_device(): summed = lax.psum(tile, 'gy')  120 us
    squeeze x1, local copies, waits for them, and re-layouts, per_device(): stiff = jnp.diagonal(local_block[0], axis1=1, axis2=2).astype(jnp.float32)  44.1 us
    all_gather x1, blocking collectives, per_device(): lax.all_gather(part, 'gx', axis=0, tiled=True)  23 us
    dot_general x1, matrix products, per_device(): jnp.einsum('snr,snq->srq', coupling[0], coupling[0], preferred_element_ty...  13.6 us
    dot_general x1, matrix products, per_device(): jnp.einsum('srk,srl->kl', basis, image, preferred_element_type=jnp.float32)  10.2 us
    gather x2, local copies, waits for them, and re-layouts, per_device(): stiff = jnp.diagonal(local_block[0], axis1=1, axis2=2).astype(jnp.float32)  6.53 us
  transfers between devices with their start and end apart: 1, of which 1 were waited for; matrix products, arithmetic and copies ran while one was open for 0% of the time, Pallas kernels for 0%

commit v1 on v0

--- a/solution.py
+++ b/solution.py
@@ -10,6 +10,20 @@
 
 
 def per_device(coupling, local_block, counts, primal, partner):
+
+    def take_joints(view):
+        along_axis = "gy"
+        workers = lax.axis_size(along_axis)
+        val, s_next = (view, 0)
+        while 1 << s_next < workers:
+            z1 = range(workers)
+            y1 = map(lambda ix: (ix, ix ^ 1 << s_next), z1)
+            t_next = list(y1)
+            everything = lax.ppermute(val, along_axis, t_next)
+            val = val + everything
+            s_next = s_next + 1
+        return val
+
     column = lax.axis_index("gx")
     stiff = jnp.diagonal(local_block[0], axis1=1, axis2=2).astype(jnp.float32)
     total = stiff
@@ -37,7 +51,7 @@
         jnp.bfloat16
     )
     tile = jnp.einsum("srk,srl->kl", basis, image, preferred_element_type=jnp.float32)
-    summed = lax.psum(tile, "gy")
+    summed = take_joints(tile)
     scale = 1.0 / jnp.sqrt(jnp.mean(jnp.abs(summed), axis=1) + 1e-06)
     result = summed * scale[:, None] * scale[None, :]
     return result[None]

time: 241 us -> 213 us (0.88)
  the two profiles are of different devices: /device:TPU:1 before, /device:TPU:6 now
where the time goes in v1:
time: 213 us; the launch traced here: 210 us
  waiting for transfers between devices  94.8 us (45%)
  local copies, waits for them, and re-layouts  53.6 us (25%)
  blocking collectives  28.3 us (13%)
  matrix products  22.5 us (11%)
  starting transfers between devices  7.62 us (4%)
  other arithmetic  3.33 us (2%)
    ppermute x5, waiting for transfers between devices, take_joints(): everything = lax.ppermute(val, along_axis, t_next)  94.8 us
    squeeze x1, local copies, waits for them, and re-layouts, per_device(): stiff = jnp.diagonal(local_block[0], axis1=1, axis2=2).astype(jnp.float32)  45.1 us
    all_gather x1, blocking collectives, per_device(): lax.all_gather(part, 'gx', axis=0, tiled=True)  28.3 us
    dot_general x1, matrix products, per_device(): jnp.einsum('snr,snq->srq', coupling[0], coupling[0], preferred_element_ty...  13.5 us
    ppermute x5, starting transfers between devices, take_joints(): everything = lax.ppermute(val, along_axis, t_next)  7.62 us
    gather x2, local copies, waits for them, and re-layouts, per_device(): stiff = jnp.diagonal(local_block[0], axis1=1, axis2=2).astype(jnp.float32)  6.55 us
    dot_general x1, matrix products, per_device(): jnp.einsum('srq,sqk->srk', schur, basis, preferred_element_type=jnp.float32)  6.1 us
  transfers between devices with their start and end apart: 5, of which 5 were waited for; matrix products, arithmetic and copies ran while one was open for 0% of the time, Pallas kernels for 0%

profile of v1, /device:TPU:6, one launch (start us, length us, event | category | flops | bytes accessed | tf_op | source)
XLA Modules:
  0.0 210.2 jit_solution(6395172215831171771)
XLA Ops:
  0.0 0.0 copy-start
  0.0 45.1 %copy.22 = bf16[8,512,512]{0,2,1:T(8,128)(2,1)} copy(bf16[8,512,512]{2,1,0:T(8,128)(2,1)} %bitcast.42) | data formatting | bytes 8388608 | tf_op jit(solution)/shard_map/squeeze | solution.py:28
  45.1 6.5 %gather_fusion = bf16[512,8]{1,0:T(8,128)(2,1)S(1)} fusion(bf16[8,512,512]{0,2,1:T(8,128)(2,1)} %copy.22, s32[512]{0:T(512)S(1)} %bitcast.41), kind=kCustom, calls=%fused_computation | custom fusion | bytes 20480 | tf_op jit(solution)/shard_map/jit(diagonal)/gather | solution.py:28
  51.6 0.1 copy.23
  51.7 28.3 %all-gather = f32[64,512]{1,0:T(8,128)S(1)} all-gather(f32[8,512]{1,0:T(8,128)S(1)} %convert_bitcast_fusion), channel_id=2, replica_groups=mesh['gx'=8,'gy'=32] {'gx'}, dimensions={0}, use_global_device_ids=true | all-gather | bytes 147456 | tf_op jit(solution)/shard_map/all_gather | solution.py:33
  80.0 0.6 constant_dynamic-slice_fusion
  80.6 0.6 iota_compare_fusion.4
  81.1 0.0 copy-start.2
  81.1 0.0 copy-start.1
  81.2 13.5 %fusion = f32[8,512,512]{2,1,0:T(8,128)} fusion(bf16[1,8,1024,512]{3,2,1,0:T(8,128)(2,1)} %param.5), kind=kOutput, calls=%fused_computation.1 | convolution fusion | flops 4294967296 | bytes 16777216 | tf_op jit(solution)/shard_map/snr,snq->srq/dot_general | solution.py:44
  94.7 0.1 fusion.21
  94.8 1.3 iota_compare_fusion.2
  96.1 0.1 fusion.18
  96.2 6.1 %fusion.29 = bf16[8,512,512]{2,1,0:T(8,128)(2,1)S(1)} fusion(f32[8,512,512]{2,1,0:T(8,128)} %fusion, f32[8,512]{1,0:T(8,128)S(1)} %fusion.21, bf16[8,512]{1,0:T(8,128)(2,1)S(1)} %add_divide_fusion, s32[8,512]{1,0:T(8,128)S(1)} %bitcast.43, bf16[1,8,512,512]{3,2,1,0:T(8,128)(2,1)} %param.6), kind=kOutput, calls=%fused_computation.8.clone.clone.clone.2 | convolution fusion | flops 2164260864 | bytes 16818176 | tf_op jit(solution)/shard_map/srq,sqk->srk/dot_general | solution.py:50
  102.3 2.9 %fusion.15 = f32[512,512]{0,1:T(8,128)S(1)} fusion(bf16[8,512]{1,0:T(8,128)(2,1)S(1)} %add_divide_fusion, s32[8,512]{1,0:T(8,128)S(1)} %bitcast.44, bf16[8,512,512]{2,1,0:T(8,128)(2,1)S(1)} %fusion.29), kind=kOutput, calls=%fused_computation.14 | convolution fusion | flops 2151677952 | bytes 5267456 | tf_op jit(solution)/shard_map/srk,srl->kl/dot_general | solution.py:53
  105.2 0.1 collective-permute-start
  105.3 2.6 %collective-permute-done = f32[512,512]{0,1:T(8,128)S(1)} collective-permute-done((f32[512,512]{0,1:T(8,128)S(1)}, f32[512,512]{0,1:T(8,128)S(1)}, u32[]{:S(2)}, u32[]{:S(2)}) %collective-permute-start) | collective-permute-done | bytes 1048608 | tf_op jit(solution)/shard_map/ppermute | solution.py:22
  107.9 0.2 add.63
  108.2 0.9 collective-permute-start.1
  109.1 24.4 %collective-permute-done.1 = f32[512,512]{0,1:T(8,128)S(1)} collective-permute-done((f32[512,512]{0,1:T(8,128)S(1)}, f32[512,512]{0,1:T(8,128)S(1)}, u32[]{:S(2)}, u32[]{:S(2)}) %collective-permute-start.1) | collective-permute-done | bytes 1048608 | tf_op jit(solution)/shard_map/ppermute | solution.py:22
  133.4 0.2 add.64
  133.7 1.7 collective-permute-start.2
  135.3 24.5 %collective-permute-done.2 = f32[512,512]{0,1:T(8,128)S(1)} collective-permute-done((f32[512,512]{0,1:T(8,128)S(1)}, f32[512,512]{0,1:T(8,128)S(1)}, u32[]{:S(2)}, u32[]{:S(2)}) %collective-permute-start.2) | collective-permute-done | bytes 1048608 | tf_op jit(solution)/shard_map/ppermute | solution.py:22
  159.8 0.2 add.65
  160.0 1.7 collective-permute-start.3
  161.7 21.9 %collective-permute-done.3 = f32[512,512]{0,1:T(8,128)S(1)} collective-permute-done((f32[512,512]{0,1:T(8,128)S(1)}, f32[512,512]{0,1:T(8,128)S(1)}, u32[]{:S(2)}, u32[]{:S(2)}) %collective-permute-start.3) | collective-permute-done | bytes 1048608 | tf_op jit(solution)/shard_map/ppermute | solution.py:22
  183.5 0.2 add.66
  183.8 3.3 %collective-permute-start.4 = (f32[512,512]{0,1:T(8,128)S(1)}, f32[512,512]{0,1:T(8,128)S(1)}, u32[]{:S(2)}, u32[]{:S(2)}) collective-permute-start(f32[512,512]{0,1:T(8,128)S(1)} %add.66), channel_id=1, source_target_pairs={{0,16},{1,17},{2,18},{3,19},{4,20},{5,21},{6,22},{7,23},{8,24},{9,... | collective-permute-start | bytes 3145736 | tf_op jit(solution)/shard_map/ppermute | solution.py:22
  187.0 21.4 %collective-permute-done.4 = f32[512,512]{0,1:T(8,128)S(1)} collective-permute-done((f32[512,512]{0,1:T(8,128)S(1)}, f32[512,512]{0,1:T(8,128)S(1)}, u32[]{:S(2)}, u32[]{:S(2)}) %collective-permute-start.4) | collective-permute-done | bytes 1048608 | tf_op jit(solution)/shard_map/ppermute | solution.py:22
  208.5 0.3 abs_reduce_fusion
  208.8 0.2 multiply_bitcast_fusion
  208.9 1.3 copy.26
  (8 shorter events, 0.0 us)
Async XLA Ops:
  0.0 80.0 %copy-start = (s32[3,8]{1,0:T(4,128)S(1)}, s32[3,8]{1,0:T(4,128)}, u32[]{:S(2)}) copy-start(s32[3,8]{1,0:T(4,128)} %param.9) | copy-start | bytes 292
  81.1 13.6 %copy-start.2 = (s32[1,8]{1,0:T(1,128)S(1)}, s32[1,8]{1,0:T(1,128)}, u32[]{:S(2)}) copy-start(s32[1,8]{1,0:T(1,128)} %param.7) | copy-start | bytes 100
  81.1 15.0 %copy-start.1 = (s32[1,8,512]{2,1,0:T(8,128)S(1)}, s32[1,8,512]{2,1,0:T(8,128)}, u32[]{:S(2)}) copy-start(s32[1,8,512]{2,1,0:T(8,128)} %param.8) | copy-start | bytes 49156
  105.2 2.7 %collective-permute-start = (f32[512,512]{0,1:T(8,128)S(1)}, f32[512,512]{0,1:T(8,128)S(1)}, u32[]{:S(2)}, u32[]{:S(2)}) collective-permute-start(f32[512,512]{0,1:T(8,128)S(1)} %fusion.15), channel_id=1, source_target_pairs={{0,1},{1,0},{2,3},{3,2},{4,5},{5,4},{6,7},{7,6},{8,9},{9,8},{10,11... | collective-permute-start | bytes 3145736 | tf_op jit(solution)/shard_map/ppermute | solution.py:22
  108.2 25.3 %collective-permute-start.1 = (f32[512,512]{0,1:T(8,128)S(1)}, f32[512,512]{0,1:T(8,128)S(1)}, u32[]{:S(2)}, u32[]{:S(2)}) collective-permute-start(f32[512,512]{0,1:T(8,128)S(1)} %add.63), channel_id=1, source_target_pairs={{0,2},{1,3},{2,0},{3,1},{4,6},{5,7},{6,4},{7,5},{8,10},{9,11},{10,... | collective-permute-start | bytes 3145736 | tf_op jit(solution)/shard_map/ppermute | solution.py:22
  133.7 26.1 %collective-permute-start.2 = (f32[512,512]{0,1:T(8,128)S(1)}, f32[512,512]{0,1:T(8,128)S(1)}, u32[]{:S(2)}, u32[]{:S(2)}) collective-permute-start(f32[512,512]{0,1:T(8,128)S(1)} %add.64), channel_id=1, source_target_pairs={{0,4},{1,5},{2,6},{3,7},{4,0},{5,1},{6,2},{7,3},{8,12},{9,13},{10,... | collective-permute-start | bytes 3145736 | tf_op jit(solution)/shard_map/ppermute | solution.py:22
  160.0 23.5 %collective-permute-start.3 = (f32[512,512]{0,1:T(8,128)S(1)}, f32[512,512]{0,1:T(8,128)S(1)}, u32[]{:S(2)}, u32[]{:S(2)}) collective-permute-start(f32[512,512]{0,1:T(8,128)S(1)} %add.65), channel_id=1, source_target_pairs={{0,8},{1,9},{2,10},{3,11},{4,12},{5,13},{6,14},{7,15},{8,0},{9,1},... | collective-permute-start | bytes 3145736 | tf_op jit(solution)/shard_map/ppermute | solution.py:22
  183.8 24.7 %collective-permute-start.4 = (f32[512,512]{0,1:T(8,128)S(1)}, f32[512,512]{0,1:T(8,128)S(1)}, u32[]{:S(2)}, u32[]{:S(2)}) collective-permute-start(f32[512,512]{0,1:T(8,128)S(1)} %add.66), channel_id=1, source_target_pairs={{0,16},{1,17},{2,18},{3,19},{4,20},{5,21},{6,22},{7,23},{8,24},{9,... | collective-permute-start | bytes 3145736 | tf_op jit(solution)/shard_map/ppermute | solution.py:22
